TPU v7x, 512 devices: a whole 4x4x16 slice. The times are simulated.
512 devices in a mesh: dp: 32 (over z, x_hi), lon: 16 (over y, x_lo, core).
Axes of the slice: x: 4 (x_hi: 2, x_lo: 2; x = x_hi * 2 + x_lo), y: 4, z: 16, core: 2. Of those that a mesh axis runs over, the one named last changes fastest.
Arguments:
- fields: bfloat16 [32, 128, 48, 768], P('dp', 'lon'), may hold values from -6 to 6
- cotangent: bfloat16 [32, 128, 48, 768], P('dp', 'lon'), may hold values from -6 to 6
- first_weight: bfloat16 [2, 8, 96, 96], replicated, may hold values from -0.4375 to 0.4375
- second_weight: bfloat16 [2, 8, 96, 96], replicated, may hold values from -0.4375 to 0.4375
Outputs:
- layer_out: bfloat16 [32, 128, 48, 768], P('dp', 'lon')
- field_grad: bfloat16 [32, 128, 48, 768], P('dp', 'lon')
- first_grad: float32 [2, 8, 96, 96], replicated
- second_grad: float32 [2, 8, 96, 96], replicated
All inputs are finite; a program needn't handle non-finite values.
Results may differ from a plain program's by a relative error of at most 0.015.
Values may be sent and summed in bfloat16 or wider, within the bound.
A program may use at most 64 MiB of HBM per device.

v0:
```python
import math
import jax
import jax.numpy as jnp
from jax import lax
from jax.sharding import PartitionSpec as P

COEF = 0.7978845608028654
CUBIC = 0.044715


def gelu_value(inner):
    hyper = jnp.tanh(COEF * (inner + CUBIC * inner * inner * inner))
    return 0.5 * inner * (1.0 + hyper)


def gelu_slope(inner):
    hyper = jnp.tanh(COEF * (inner + CUBIC * inner * inner * inner))
    return 0.5 * (1.0 + hyper) + 0.5 * inner * (1.0 - hyper * hyper) * COEF * (
        1.0 + 3.0 * CUBIC * inner * inner
    )


def make_basis(length, count):
    cell_idx = jnp.arange(length, dtype=jnp.int32)
    mode_idx = jnp.arange(count, dtype=jnp.int32)
    product = cell_idx[:, None] * mode_idx[None, :] % length
    angle = product.astype(jnp.float32) * jnp.float32(2.0 * math.pi / length)
    return jnp.stack([jnp.cos(angle), -jnp.sin(angle)], axis=-1).astype(jnp.bfloat16)


def lat_apply(spec, table, lat_scale):
    return (
        jnp.einsum("kphc,phqj->kqjc", spec, table, preferred_element_type=jnp.float32) * lat_scale
    ).astype(jnp.bfloat16)


def forward_weight(weight):
    return jnp.stack([jnp.stack([weight[0], weight[1]]), jnp.stack([-weight[1], weight[0]])])


def adjoint_weight(weight):
    return jnp.stack([jnp.stack([weight[0], -weight[1]]), jnp.stack([weight[1], weight[0]])])


def block_product(spec, stacked):
    return jnp.einsum("kphbi,pqbij->kqhbj", spec, stacked, preferred_element_type=jnp.float32)


def block_adjoint(spec, stacked):
    return jnp.einsum("kphbj,pqbij->kqhbi", spec, stacked, preferred_element_type=jnp.float32)


def block_outer(left, right):
    pairs = jnp.einsum("kphbi,kqhbj->pqbij", left, right, preferred_element_type=jnp.float32)
    return jnp.stack([pairs[0, 0] + pairs[1, 1], pairs[0, 1] - pairs[1, 0]])


def on_device(fields, cotangent, first_weight, second_weight):
    cell_rows = fields[0]
    cot_rows = cotangent[0]
    lat_rows = cell_rows.shape[1]
    channels = cell_rows.shape[2]
    groups = first_weight.shape[1]
    group_width = first_weight.shape[2]
    lon_count = lax.axis_size("lon")
    total_cells = cell_rows.shape[0] * lon_count
    dft_basis = make_basis(total_cells, total_cells // 2)
    lat_basis = make_basis(lat_rows, lat_rows)
    cos_tab = lat_basis[:, :, 0]
    sin_tab = lat_basis[:, :, 1]
    lat_fwd_table = jnp.stack(
        [jnp.stack([cos_tab, sin_tab], axis=1), jnp.stack([-sin_tab, cos_tab], axis=1)], axis=0
    )
    lat_inv_table = jnp.stack(
        [jnp.stack([cos_tab.T, -sin_tab.T], axis=1), jnp.stack([sin_tab.T, cos_tab.T], axis=1)],
        axis=0,
    )
    norm_scale = 1.0 / math.sqrt(total_cells)
    lat_scale = 1.0 / math.sqrt(lat_rows)
    local_modes = cell_rows.shape[0] // 2
    mode_idx = lax.axis_index("lon") * local_modes + jnp.arange(local_modes, dtype=jnp.int32)
    mode_weight = jnp.where(mode_idx == 0, 1.0, 2.0).astype(jnp.bfloat16)[:, None, None, None]
    first_fwd = forward_weight(first_weight)
    second_fwd = forward_weight(second_weight)
    first_adj = adjoint_weight(first_weight)
    second_adj = adjoint_weight(second_weight)

    def local_dft(all_lines):
        return (
            jnp.einsum("whc,wkp->kphc", all_lines, dft_basis, preferred_element_type=jnp.float32)
            * norm_scale
        ).astype(jnp.bfloat16)

    def local_idft(all_modes):
        return (
            jnp.einsum("kphc,wkp->whc", all_modes, dft_basis, preferred_element_type=jnp.float32)
            * norm_scale
        ).astype(jnp.bfloat16)

    def lines_to_modes(all_lines):
        return lax.all_to_all(local_dft(all_lines), "lon", split_axis=0, concat_axis=3, tiled=True)

    def modes_to_lines(all_modes):
        return lax.all_to_all(local_idft(all_modes), "lon", split_axis=0, concat_axis=2, tiled=True)

    def to_spectrum(grid_rows):
        return lines_to_modes(
            lax.all_to_all(grid_rows, "lon", split_axis=2, concat_axis=0, tiled=True)
        )

    def to_cells(spec_rows):
        return modes_to_lines(
            lax.all_to_all(spec_rows, "lon", split_axis=3, concat_axis=0, tiled=True)
        )

    def split_groups(spec_rows):
        return spec_rows.reshape(local_modes, 2, lat_rows, groups, group_width)

    def join_groups(spec_rows):
        return spec_rows.astype(jnp.bfloat16).reshape(local_modes, 2, lat_rows, channels)

    lon_spec = to_spectrum(cell_rows)
    spectrum = split_groups(lat_apply(lon_spec, lat_fwd_table, lat_scale))
    inner = block_product(spectrum, first_fwd)
    act = gelu_value(inner).astype(jnp.bfloat16)
    mixed = join_groups(block_product(act, second_fwd)) * mode_weight
    mixed_lon = lat_apply(mixed, lat_inv_table, lat_scale)
    wave = to_cells(mixed_lon)
    dual_lon = to_spectrum(cot_rows)
    dual = split_groups(lat_apply(dual_lon, lat_fwd_table, lat_scale) * mode_weight)
    back = block_adjoint(dual, second_adj)
    pre = (back * gelu_slope(inner)).astype(jnp.bfloat16)
    back_spec = join_groups(block_adjoint(pre, first_adj))
    back_lon = lat_apply(back_spec, lat_inv_table, lat_scale)
    pull = to_cells(back_lon)
    layer_out = (cell_rows.astype(jnp.float32) + wave.astype(jnp.float32)).astype(jnp.bfloat16)
    field_grad = (cot_rows.astype(jnp.float32) + pull.astype(jnp.float32)).astype(jnp.bfloat16)
    sample_count = lax.axis_size("dp")
    second_term = block_outer(act, dual) / sample_count
    first_term = block_outer(spectrum, pre) / sample_count
    first_grad, second_grad = lax.psum((first_term, second_term), ("dp", "lon"))
    return (layer_out[None], field_grad[None], first_grad, second_grad)


def solution(mesh):
    placed = (P("dp", "lon", None, None), P("dp", "lon", None, None), P(), P())
    return jax.shard_map(
        on_device,
        mesh=mesh,
        in_specs=placed,
        out_specs=(P("dp", "lon", None, None), P("dp", "lon", None, None), P(), P()),
        check_vma=False,
    )
```

profile of v0, /device:TPU:1, one launch (start us, length us, event | category | flops | bytes accessed | tf_op | source)
XLA Modules:
  0.0 643.6 jit_solution(1187848861176454927)
XLA Ops:
  9.3 3.1 reshape.309
  12.4 11.0 %all-to-all-start = ((bf16[16,2,9216]{2,1,0:T(2,128)(2,1)}), bf16[16,2,9216]{2,1,0:T(2,128)(2,1)}, u32[]{:S(2)}, u32[]{:S(2)}) async-start(bf16[16,2,9216]{2,1,0:T(2,128)(2,1)} %reshape.309), calls=%async_computation | async-start | bytes 1179648 | tf_op jit(solution)/shard_map/all_to_all | solution.py:108
  24.6 3.1 reshape.317
  30.0 4.0 all-to-all-done
  34.1 5.2 all-to-all-start.4
  40.8 2.4 reshape.310
  47.2 3.1 reshape.311
  50.3 6.4 %all-to-all-start.1 = ((bf16[16,2,9216]{2,1,0:T(2,128)(2,1)}), bf16[16,2,9216]{2,1,0:T(2,128)(2,1)}, u32[]{:S(2)}, u32[]{:S(2)}) async-start(bf16[16,2,9216]{2,1,0:T(2,128)(2,1)} %reshape.311), calls=%async_computation.1 | async-start | bytes 1179648 | tf_op jit(solution)/shard_map/all_to_all | solution.py:101
  65.4 3.1 reshape.319
  68.5 5.9 all-to-all-start.5
  77.1 2.4 reshape.312
  85.0 2.4 reshape.320
  89.7 2.9 reshape.288
  101.3 3.1 reshape.321
  104.4 4.5 all-to-all-start.6
  115.7 4.1 reshape.313
  121.4 5.8 all-to-all-start.2
  135.6 3.1 reshape.323
  138.7 5.7 all-to-all-start.7
  151.4 3.1 reshape.315
  154.5 451.1 %all-reduce.3.cloned.1.call-done = (f32[2,8,96,96]{2,3,1,0:T(8,128)}, f32[2,8,96,96]{2,3,1,0:T(8,128)}) async-done(((f32[2,8,96,96]{2,3,1,0:T(8,128)}, f32[2,8,96,96]{2,3,1,0:T(8,128)}), (f32[2,8,96,96]{2,3,1,0:T(8,128)}, f32[2,8,96,96]{2,3,1,0:T(8,128)})) %all-reduce.3.cloned.1.call-update) | async-done | bytes 1179664 | tf_op jit(solution)/shard_map/psum | solution.py:141
  609.2 7.4 %all-to-all-start.3 = ((bf16[16,2,9216]{2,1,0:T(2,128)(2,1)}), bf16[16,2,9216]{2,1,0:T(2,128)(2,1)}, u32[]{:S(2)}, u32[]{:S(2)}) async-start(bf16[16,2,9216]{2,1,0:T(2,128)(2,1)} %reshape.315), calls=%async_computation.3 | async-start | bytes 1179648 | tf_op jit(solution)/shard_map/all_to_all | solution.py:104
  616.6 2.4 reshape.324
  627.1 2.4 reshape.316
  (147 shorter events, 80.4 us)
Async XLA Ops:
  12.3 11.0 %copy-start = (bf16[1,8,48,768]{3,2,1,0:T(8,128)(2,1)S(1)}, bf16[1,8,48,768]{3,2,1,0:T(8,128)(2,1)}, u32[]{:S(2)}) copy-start(bf16[1,8,48,768]{3,2,1,0:T(8,128)(2,1)} %param.5) | copy-start | bytes 1769476
  12.4 21.7 %all-to-all-start = ((bf16[16,2,9216]{2,1,0:T(2,128)(2,1)}), bf16[16,2,9216]{2,1,0:T(2,128)(2,1)}, u32[]{:S(2)}, u32[]{:S(2)}) async-start(bf16[16,2,9216]{2,1,0:T(2,128)(2,1)} %reshape.309), calls=%async_computation | async-start | bytes 1179648 | tf_op jit(solution)/shard_map/all_to_all | solution.py:108
  24.6 15.4 %copy-start.21 = (bf16[2,8,96,96]{3,2,1,0:T(8,128)(2,1)S(1)}, bf16[2,8,96,96]{3,2,1,0:T(8,128)(2,1)}, u32[]{:S(2)}) copy-start(bf16[2,8,96,96]{3,2,1,0:T(8,128)(2,1)} %param.6) | copy-start | bytes 884740
  34.1 16.2 %all-to-all-start.4 = ((bf16[16,2,9216]{2,1,0:T(2,128)(2,1)}), bf16[16,2,9216]{2,1,0:T(2,128)(2,1)}, u32[]{:S(2)}, u32[]{:S(2)}) async-start(bf16[16,2,9216]{2,1,0:T(2,128)(2,1)} %reshape.317), calls=%async_computation.4 | async-start | bytes 1179648 | tf_op jit(solution)/shard_map/all_to_all | solution.py:108
  47.2 9.6 %copy-start.29 = (bf16[48,1,48]{2,0,1:T(8,128)(2,1)S(1)}, bf16[48,1,48]{2,0,1:T(8,128)(2,1)}, u32[]{:S(2)}) copy-start(bf16[48,1,48]{2,0,1:T(8,128)(2,1)} %get-tuple-element.48) | copy-start | bytes 13828
  47.2 9.6 %copy-start.30 = (bf16[48,1,48]{2,0,1:T(8,128)(2,1)S(1)}, bf16[48,1,48]{2,0,1:T(8,128)(2,1)}, u32[]{:S(2)}) copy-start(bf16[48,1,48]{2,0,1:T(8,128)(2,1)} %get-tuple-element.49) | copy-start | bytes 13828
  47.2 9.6 %copy-start.31 = (bf16[48,1,48]{2,0,1:T(8,128)(2,1)S(1)}, bf16[48,1,48]{2,0,1:T(8,128)(2,1)}, u32[]{:S(2)}) copy-start(bf16[48,1,48]{2,0,1:T(8,128)(2,1)} %fusion.91) | copy-start | bytes 13828
  47.2 10.2 %copy-start.22 = (bf16[2,8,96,96]{3,2,1,0:T(8,128)(2,1)S(1)}, bf16[2,8,96,96]{3,2,1,0:T(8,128)(2,1)}, u32[]{:S(2)}) copy-start(bf16[2,8,96,96]{3,2,1,0:T(8,128)(2,1)} %param.7) | copy-start | bytes 884740
  50.3 18.2 %all-to-all-start.1 = ((bf16[16,2,9216]{2,1,0:T(2,128)(2,1)}), bf16[16,2,9216]{2,1,0:T(2,128)(2,1)}, u32[]{:S(2)}, u32[]{:S(2)}) async-start(bf16[16,2,9216]{2,1,0:T(2,128)(2,1)} %reshape.311), calls=%async_computation.1 | async-start | bytes 1179648 | tf_op jit(solution)/shard_map/all_to_all | solution.py:101
  65.4 9.5 %copy-start.8 = (bf16[1,8,96,96]{3,2,0,1:T(8,128)(2,1)S(1)}, bf16[1,8,96,96]{3,2,0,1:T(8,128)(2,1)}, u32[]{:S(2)}) copy-start(bf16[1,8,96,96]{3,2,0,1:T(8,128)(2,1)} %get-tuple-element.26) | copy-start | bytes 442372
  65.4 9.5 %copy-start.9 = (bf16[1,8,96,96]{3,2,0,1:T(8,128)(2,1)S(1)}, bf16[1,8,96,96]{3,2,0,1:T(8,128)(2,1)}, u32[]{:S(2)}) copy-start(bf16[1,8,96,96]{3,2,0,1:T(8,128)(2,1)} %get-tuple-element.27) | copy-start | bytes 442372
  65.4 9.5 %copy-start.10 = (bf16[1,8,96,96]{3,2,0,1:T(8,128)(2,1)S(1)}, bf16[1,8,96,96]{3,2,0,1:T(8,128)(2,1)}, u32[]{:S(2)}) copy-start(bf16[1,8,96,96]{3,2,0,1:T(8,128)(2,1)} %get-tuple-element.28) | copy-start | bytes 442372
  68.5 7.5 %copy-start.11 = (bf16[1,8,96,96]{3,2,0,1:T(8,128)(2,1)S(1)}, bf16[1,8,96,96]{3,2,0,1:T(8,128)(2,1)}, u32[]{:S(2)}) copy-start(bf16[1,8,96,96]{3,2,0,1:T(8,128)(2,1)} %get-tuple-element.31) | copy-start | bytes 442372
  68.5 7.5 %copy-start.12 = (bf16[1,8,96,96]{3,2,0,1:T(8,128)(2,1)S(1)}, bf16[1,8,96,96]{3,2,0,1:T(8,128)(2,1)}, u32[]{:S(2)}) copy-start(bf16[1,8,96,96]{3,2,0,1:T(8,128)(2,1)} %get-tuple-element.32) | copy-start | bytes 442372
  68.5 7.5 %copy-start.13 = (bf16[1,8,96,96]{3,2,0,1:T(8,128)(2,1)S(1)}, bf16[1,8,96,96]{3,2,0,1:T(8,128)(2,1)}, u32[]{:S(2)}) copy-start(bf16[1,8,96,96]{3,2,0,1:T(8,128)(2,1)} %get-tuple-element.33) | copy-start | bytes 442372
  68.5 16.5 %all-to-all-start.5 = ((bf16[16,2,9216]{2,1,0:T(2,128)(2,1)}), bf16[16,2,9216]{2,1,0:T(2,128)(2,1)}, u32[]{:S(2)}, u32[]{:S(2)}) async-start(bf16[16,2,9216]{2,1,0:T(2,128)(2,1)} %reshape.319), calls=%async_computation.5 | async-start | bytes 1179648 | tf_op jit(solution)/shard_map/all_to_all | solution.py:101
  89.7 2.9 copy-start.28
  89.7 2.9 copy-start.32
  101.3 7.6 %copy-start.3 = (bf16[2,8,96,96]{3,2,0,1:T(8,128)(2,1)S(1)}, bf16[2,8,96,96]{3,2,0,1:T(8,128)(2,1)}, u32[]{:S(2)}) copy-start(bf16[2,8,96,96]{3,2,0,1:T(8,128)(2,1)} %copy-done.2) | copy-start | bytes 884740
  104.4 17.0 %all-to-all-start.6 = ((bf16[16,2,9216]{2,1,0:T(2,128)(2,1)}), bf16[16,2,9216]{2,1,0:T(2,128)(2,1)S(1)}, u32[]{:S(2)}, u32[]{:S(2)}) async-start(bf16[16,2,9216]{2,1,0:T(2,128)(2,1)} %reshape.321), calls=%async_computation.6 | async-start | bytes 1179648 | tf_op jit(solution)/shard_map/all_to_all | solution.py:113
  121.4 17.3 %all-to-all-start.2 = ((bf16[16,2,9216]{2,1,0:T(2,128)(2,1)}), bf16[16,2,9216]{2,1,0:T(2,128)(2,1)}, u32[]{:S(2)}, u32[]{:S(2)}) async-start(bf16[16,2,9216]{2,1,0:T(2,128)(2,1)} %reshape.313), calls=%async_computation.2 | async-start | bytes 1179648 | tf_op jit(solution)/shard_map/all_to_all | solution.py:113
  127.2 478.5 %all-reduce.3.cloned.1.call-start = ((), (), s32[]{:S(2)}) async-start(), calls=%async_computation.8 | async-start | bytes 3145728 | tf_op jit(solution)/shard_map/psum | solution.py:141
  138.7 470.5 %all-to-all-start.7 = ((bf16[16,2,9216]{2,1,0:T(2,128)(2,1)}), bf16[16,2,9216]{2,1,0:T(2,128)(2,1)}, u32[]{:S(2)}, u32[]{:S(2)}) async-start(bf16[16,2,9216]{2,1,0:T(2,128)(2,1)} %reshape.323), calls=%async_computation.7 | async-start | bytes 1179648 | tf_op jit(solution)/shard_map/all_to_all | solution.py:104
  609.2 17.9 %all-to-all-start.3 = ((bf16[16,2,9216]{2,1,0:T(2,128)(2,1)}), bf16[16,2,9216]{2,1,0:T(2,128)(2,1)}, u32[]{:S(2)}, u32[]{:S(2)}) async-start(bf16[16,2,9216]{2,1,0:T(2,128)(2,1)} %reshape.315), calls=%async_computation.3 | async-start | bytes 1179648 | tf_op jit(solution)/shard_map/all_to_all | solution.py:104
  (18 other events, 25.7 us)
Sparse Core Ops, SparseCore 0:
  133.9 471.6 all-reduce.2
where the time goes:
time: 652 us; the launch traced here: 644 us
  waiting for transfers between devices  458 us (70%)
  local copies, waits for them, and re-layouts  88.6 us (14%)
  starting transfers between devices  52 us (8%)
  other arithmetic  17.4 us (3%)
  between operations  15.2 us (2%)
  matrix products  12.2 us (2%)
    psum x1, waiting for transfers between devices, on_device(): first_grad, second_grad = lax.psum((first_term, second_term), ('dp', 'lon'))  451 us
    unnamed x90, local copies, waits for them, and re-layouts  52.7 us
    all_to_all x2, starting transfers between devices, to_spectrum(): lax.all_to_all(grid_rows, 'lon', split_axis=2, concat_axis=0, tiled=True)  16.1 us
    all_to_all x2, starting transfers between devices, modes_to_lines(): lax.all_to_all(local_idft(all_modes), 'lon', split_axis=0, concat_axis=2,...  13.2 us
  transfers between devices with their start and end apart: 9, of which 4 were waited for; matrix products, arithmetic and copies ran while one was open for 13% of the time, Pallas kernels for 0%

commit v1 on v0

--- a/solution.py
+++ b/solution.py
@@ -6,6 +6,11 @@
 
 COEF = 0.7978845608028654
 CUBIC = 0.044715
+
+
+def begin_the_core(body):
+    right_arr = lax.psum(lax.psum(body, "dp"), "lon")
+    return right_arr
 
 
 def gelu_value(inner):
@@ -138,7 +143,7 @@
     sample_count = lax.axis_size("dp")
     second_term = block_outer(act, dual) / sample_count
     first_term = block_outer(spectrum, pre) / sample_count
-    first_grad, second_grad = lax.psum((first_term, second_term), ("dp", "lon"))
+    first_grad, second_grad = begin_the_core((first_term, second_term))
     return (layer_out[None], field_grad[None], first_grad, second_grad)
 
 

time: 652 us -> 605 us (0.928)
  waiting for transfers between devices: 458 us -> 409 us
    psum x1 -> x2, waiting for transfers between devices: 451 us -> 401 us  [begin_the_core(): right_arr = lax.psum(lax.psum(body, 'dp'), 'lon')]
    unnamed x90 -> x98, local copies, waits for them, and re-layouts: 52.7 us -> 52 us
  transfers between devices with their start and end apart: 9 -> 10, of which waited for: 4 -> 5; matrix products, arithmetic and copies ran while one was open for 13% -> 15% of each run, Pallas kernels for 0% -> 0%
where the time goes in v1:
time: 605 us; the launch traced here: 597 us
  waiting for transfers between devices  409 us (68%)
  local copies, waits for them, and re-layouts  89.6 us (15%)
  starting transfers between devices  50.8 us (8%)
  other arithmetic  17.8 us (3%)
  between operations  15.3 us (3%)
  matrix products  14.4 us (2%)
    psum x2, waiting for transfers between devices, begin_the_core(): right_arr = lax.psum(lax.psum(body, 'dp'), 'lon')  401 us
    unnamed x98, local copies, waits for them, and re-layouts  52 us
    all_to_all x2, starting transfers between devices, to_spectrum(): lax.all_to_all(grid_rows, 'lon', split_axis=2, concat_axis=0, tiled=True)  16.1 us
    all_to_all x2, starting transfers between devices, lines_to_modes(): lax.all_to_all(local_dft(all_lines), 'lon', split_axis=0, concat_axis=3,...  12.3 us
  transfers between devices with their start and end apart: 10, of which 5 were waited for; matrix products, arithmetic and copies ran while one was open for 15% of the time, Pallas kernels for 0%

profile of v1, /device:TPU:1, one launch (start us, length us, event | category | flops | bytes accessed | tf_op | source)
XLA Modules:
  0.0 597.0 jit_solution(5755980012936249174)
XLA Ops:
  9.3 3.1 reshape.309
  12.4 11.0 %all-to-all-start = ((bf16[16,2,9216]{2,1,0:T(2,128)(2,1)}), bf16[16,2,9216]{2,1,0:T(2,128)(2,1)}, u32[]{:S(2)}, u32[]{:S(2)}) async-start(bf16[16,2,9216]{2,1,0:T(2,128)(2,1)} %reshape.309), calls=%async_computation | async-start | bytes 1179648 | tf_op jit(solution)/shard_map/all_to_all | solution.py:113
  24.6 3.1 reshape.317
  30.0 4.1 all-to-all-done
  34.1 5.2 all-to-all-start.4
  47.2 3.1 reshape.311
  50.3 6.4 %all-to-all-start.1 = ((bf16[16,2,9216]{2,1,0:T(2,128)(2,1)}), bf16[16,2,9216]{2,1,0:T(2,128)(2,1)}, u32[]{:S(2)}, u32[]{:S(2)}) async-start(bf16[16,2,9216]{2,1,0:T(2,128)(2,1)} %reshape.311), calls=%async_computation.1 | async-start | bytes 1179648 | tf_op jit(solution)/shard_map/all_to_all | solution.py:106
  65.4 3.1 reshape.319
  68.5 5.9 all-to-all-start.5
  89.7 2.9 reshape.288
  101.1 2.5 copy.148
  103.7 3.1 reshape.321
  106.7 5.1 all-to-all-start.6
  116.1 3.0 convolution_bitcast_fusion
  119.1 2.5 copy.132
  121.6 3.1 reshape.313
  126.2 5.8 all-to-all-start.2
  141.3 3.1 reshape.323
  144.4 5.7 all-to-all-start.7
  157.1 3.1 reshape.315
  162.3 5.2 all-to-all-start.3
  170.2 259.4 %all-reduce.5.cloned.1.call-done = (f32[2,8,96,96]{2,3,1,0:T(8,128)}, f32[2,8,96,96]{2,3,1,0:T(8,128)}) async-done(((f32[2,8,96,96]{2,3,1,0:T(8,128)}, f32[2,8,96,96]{2,3,1,0:T(8,128)}), (f32[2,8,96,96]{2,3,1,0:T(8,128)}, f32[2,8,96,96]{2,3,1,0:T(8,128)})) %all-reduce.5.cloned.1.call-update) | async-done | bytes 1179664 | tf_op jit(solution)/shard_map/psum | solution.py:12
  440.8 2.5 add_convert_fusion
  444.2 142.0 %all-reduce.7.cloned.1.call-done = (f32[2,8,96,96]{2,3,1,0:T(8,128)}, f32[2,8,96,96]{2,3,1,0:T(8,128)}) async-done(((f32[2,8,96,96]{2,3,1,0:T(8,128)}, f32[2,8,96,96]{2,3,1,0:T(8,128)}), (f32[2,8,96,96]{2,3,1,0:T(8,128)}, f32[2,8,96,96]{2,3,1,0:T(8,128)})) %all-reduce.7.cloned.1.call-update) | async-done | bytes 1179664 | tf_op jit(solution)/shard_map/psum | solution.py:12
  (158 shorter events, 88.0 us)
Async XLA Ops:
  12.3 11.0 %copy-start.1 = (bf16[1,8,48,768]{3,2,1,0:T(8,128)(2,1)S(1)}, bf16[1,8,48,768]{3,2,1,0:T(8,128)(2,1)}, u32[]{:S(2)}) copy-start(bf16[1,8,48,768]{3,2,1,0:T(8,128)(2,1)} %param.5) | copy-start | bytes 1769476
  12.4 21.7 %all-to-all-start = ((bf16[16,2,9216]{2,1,0:T(2,128)(2,1)}), bf16[16,2,9216]{2,1,0:T(2,128)(2,1)}, u32[]{:S(2)}, u32[]{:S(2)}) async-start(bf16[16,2,9216]{2,1,0:T(2,128)(2,1)} %reshape.309), calls=%async_computation | async-start | bytes 1179648 | tf_op jit(solution)/shard_map/all_to_all | solution.py:113
  24.6 15.4 %copy-start.22 = (bf16[2,8,96,96]{3,2,1,0:T(8,128)(2,1)S(1)}, bf16[2,8,96,96]{3,2,1,0:T(8,128)(2,1)}, u32[]{:S(2)}) copy-start(bf16[2,8,96,96]{3,2,1,0:T(8,128)(2,1)} %param.6) | copy-start | bytes 884740
  34.1 16.2 %all-to-all-start.4 = ((bf16[16,2,9216]{2,1,0:T(2,128)(2,1)}), bf16[16,2,9216]{2,1,0:T(2,128)(2,1)}, u32[]{:S(2)}, u32[]{:S(2)}) async-start(bf16[16,2,9216]{2,1,0:T(2,128)(2,1)} %reshape.317), calls=%async_computation.4 | async-start | bytes 1179648 | tf_op jit(solution)/shard_map/all_to_all | solution.py:113
  47.2 9.6 %copy-start.32 = (bf16[48,1,48]{2,0,1:T(8,128)(2,1)S(1)}, bf16[48,1,48]{2,0,1:T(8,128)(2,1)}, u32[]{:S(2)}) copy-start(bf16[48,1,48]{2,0,1:T(8,128)(2,1)} %get-tuple-element.50) | copy-start | bytes 13828
  47.2 9.6 %copy-start.33 = (bf16[48,1,48]{2,0,1:T(8,128)(2,1)S(1)}, bf16[48,1,48]{2,0,1:T(8,128)(2,1)}, u32[]{:S(2)}) copy-start(bf16[48,1,48]{2,0,1:T(8,128)(2,1)} %get-tuple-element.51) | copy-start | bytes 13828
  47.2 9.6 %copy-start.34 = (bf16[48,1,48]{2,0,1:T(8,128)(2,1)S(1)}, bf16[48,1,48]{2,0,1:T(8,128)(2,1)}, u32[]{:S(2)}) copy-start(bf16[48,1,48]{2,0,1:T(8,128)(2,1)} %fusion.91) | copy-start | bytes 13828
  47.2 10.2 %copy-start.23 = (bf16[2,8,96,96]{3,2,1,0:T(8,128)(2,1)S(1)}, bf16[2,8,96,96]{3,2,1,0:T(8,128)(2,1)}, u32[]{:S(2)}) copy-start(bf16[2,8,96,96]{3,2,1,0:T(8,128)(2,1)} %param.7) | copy-start | bytes 884740
  50.3 18.2 %all-to-all-start.1 = ((bf16[16,2,9216]{2,1,0:T(2,128)(2,1)}), bf16[16,2,9216]{2,1,0:T(2,128)(2,1)}, u32[]{:S(2)}, u32[]{:S(2)}) async-start(bf16[16,2,9216]{2,1,0:T(2,128)(2,1)} %reshape.311), calls=%async_computation.1 | async-start | bytes 1179648 | tf_op jit(solution)/shard_map/all_to_all | solution.py:106
  65.4 9.5 %copy-start.9 = (bf16[1,8,96,96]{3,2,0,1:T(8,128)(2,1)S(1)}, bf16[1,8,96,96]{3,2,0,1:T(8,128)(2,1)}, u32[]{:S(2)}) copy-start(bf16[1,8,96,96]{3,2,0,1:T(8,128)(2,1)} %get-tuple-element.28) | copy-start | bytes 442372
  65.4 9.5 %copy-start.10 = (bf16[1,8,96,96]{3,2,0,1:T(8,128)(2,1)S(1)}, bf16[1,8,96,96]{3,2,0,1:T(8,128)(2,1)}, u32[]{:S(2)}) copy-start(bf16[1,8,96,96]{3,2,0,1:T(8,128)(2,1)} %get-tuple-element.29) | copy-start | bytes 442372
  65.4 9.5 %copy-start.11 = (bf16[1,8,96,96]{3,2,0,1:T(8,128)(2,1)S(1)}, bf16[1,8,96,96]{3,2,0,1:T(8,128)(2,1)}, u32[]{:S(2)}) copy-start(bf16[1,8,96,96]{3,2,0,1:T(8,128)(2,1)} %get-tuple-element.30) | copy-start | bytes 442372
  68.5 7.5 %copy-start.12 = (bf16[1,8,96,96]{3,2,0,1:T(8,128)(2,1)S(1)}, bf16[1,8,96,96]{3,2,0,1:T(8,128)(2,1)}, u32[]{:S(2)}) copy-start(bf16[1,8,96,96]{3,2,0,1:T(8,128)(2,1)} %get-tuple-element.33) | copy-start | bytes 442372
  68.5 7.5 %copy-start.13 = (bf16[1,8,96,96]{3,2,0,1:T(8,128)(2,1)S(1)}, bf16[1,8,96,96]{3,2,0,1:T(8,128)(2,1)}, u32[]{:S(2)}) copy-start(bf16[1,8,96,96]{3,2,0,1:T(8,128)(2,1)} %get-tuple-element.34) | copy-start | bytes 442372
  68.5 7.5 %copy-start.14 = (bf16[1,8,96,96]{3,2,0,1:T(8,128)(2,1)S(1)}, bf16[1,8,96,96]{3,2,0,1:T(8,128)(2,1)}, u32[]{:S(2)}) copy-start(bf16[1,8,96,96]{3,2,0,1:T(8,128)(2,1)} %get-tuple-element.35) | copy-start | bytes 442372
  68.5 16.5 %all-to-all-start.5 = ((bf16[16,2,9216]{2,1,0:T(2,128)(2,1)}), bf16[16,2,9216]{2,1,0:T(2,128)(2,1)}, u32[]{:S(2)}, u32[]{:S(2)}) async-start(bf16[16,2,9216]{2,1,0:T(2,128)(2,1)} %reshape.319), calls=%async_computation.5 | async-start | bytes 1179648 | tf_op jit(solution)/shard_map/all_to_all | solution.py:106
  103.7 8.2 %copy-start.5 = (bf16[2,8,96,96]{3,2,0,1:T(8,128)(2,1)S(1)}, bf16[2,8,96,96]{3,2,0,1:T(8,128)(2,1)}, u32[]{:S(2)}) copy-start(bf16[2,8,96,96]{3,2,0,1:T(8,128)(2,1)} %copy-done.4) | copy-start | bytes 884740
  106.7 19.5 %all-to-all-start.6 = ((bf16[16,2,9216]{2,1,0:T(2,128)(2,1)}), bf16[16,2,9216]{2,1,0:T(2,128)(2,1)}, u32[]{:S(2)}, u32[]{:S(2)}) async-start(bf16[16,2,9216]{2,1,0:T(2,128)(2,1)} %reshape.321), calls=%async_computation.6 | async-start | bytes 1179648 | tf_op jit(solution)/shard_map/all_to_all | solution.py:118
  124.7 7.6 %copy-start.6 = (f32[1,8,96,96]{2,3,1,0:T(8,128)S(1)}, f32[1,8,96,96]{2,3,1,0:T(8,128)}, u32[]{:S(2)}) copy-start(f32[1,8,96,96]{2,3,1,0:T(8,128)} %fusion.70) | copy-start | bytes 884740
  126.2 18.2 %all-to-all-start.2 = ((bf16[16,2,9216]{2,1,0:T(2,128)(2,1)}), bf16[16,2,9216]{2,1,0:T(2,128)(2,1)}, u32[]{:S(2)}, u32[]{:S(2)}) async-start(bf16[16,2,9216]{2,1,0:T(2,128)(2,1)} %reshape.313), calls=%async_computation.2 | async-start | bytes 1179648 | tf_op jit(solution)/shard_map/all_to_all | solution.py:118
  132.0 297.5 %all-reduce.5.cloned.1.call-start = ((), (), s32[]{:S(2)}) async-start(), calls=%async_computation.8 | async-start | bytes 3145728 | tf_op jit(solution)/shard_map/psum | solution.py:12
  144.4 17.9 %all-to-all-start.7 = ((bf16[16,2,9216]{2,1,0:T(2,128)(2,1)}), bf16[16,2,9216]{2,1,0:T(2,128)(2,1)}, u32[]{:S(2)}, u32[]{:S(2)}) async-start(bf16[16,2,9216]{2,1,0:T(2,128)(2,1)} %reshape.323), calls=%async_computation.7 | async-start | bytes 1179648 | tf_op jit(solution)/shard_map/all_to_all | solution.py:109
  162.3 271.7 %all-to-all-start.3 = ((bf16[16,2,9216]{2,1,0:T(2,128)(2,1)}), bf16[16,2,9216]{2,1,0:T(2,128)(2,1)}, u32[]{:S(2)}, u32[]{:S(2)}) async-start(bf16[16,2,9216]{2,1,0:T(2,128)(2,1)} %reshape.315), calls=%async_computation.3 | async-start | bytes 1179648 | tf_op jit(solution)/shard_map/all_to_all | solution.py:109
  167.4 418.7 %all-reduce.7.cloned.1.call-start = ((), (), s32[]{:S(2)}) async-start(), calls=%async_computation.9 | async-start | bytes 3145728 | tf_op jit(solution)/shard_map/psum | solution.py:12
  (23 other events, 37.8 us)
Sparse Core Ops, SparseCore 0:
  136.4 293.1 all-reduce.4
  432.8 153.3 all-reduce.6
